TPU v7x, 32 devices: a whole 2x2x4 slice. The times are simulated.
32 devices in a mesh: alpha: 4 (over z), beta: 4 (over y, core), task: 2 (over x).
Axes of the slice: x: 2, y: 2, z: 4, core: 2. Of those that a mesh axis runs over, the one named last changes fastest.
Arguments:
- vector: float32 [1024, 4096], P('alpha', 'beta'), may hold values from -6 to 6
- op_alpha: float32 [2, 1024, 1024], P('task', 'alpha'), may hold values from -2 to 2, as said below
- op_beta: float32 [2, 4096, 4096], P('task', 'beta'), may hold values from -2 to 2, as said below
- op_weight: float32 [2], replicated, may hold values from 0.5 to 2
- alpha_string: int32 [1024], P('alpha'), may hold values from 0 to 65535
- beta_string: int32 [4096], P('beta'), may hold values from 0 to 65535
- alpha_energy: float32 [65536], replicated, may hold values from -4 to 4
- beta_energy: float32 [65536], replicated, may hold values from -4 to 4
Outputs:
- sigma: float32 [1024, 4096], P('alpha', ('beta', 'task'))
Inputs may be any that keep to these rules, and one draw needn't show every extreme that they name: Every op_alpha[k] is a symmetric matrix. Every op_beta[k] is a symmetric matrix.
All inputs are finite; a program needn't handle non-finite values.
Results may differ from a plain program's by a relative error of at most 0.0001.
Values sent between devices are 32-bit elements; how exact they have to be, the bound alone decides.
A program may use at most 128 MiB of HBM per device.

v0:
```python
import functools

import jax
import jax.numpy as jnp
from jax import lax
from jax.experimental import pallas as pl
from jax.experimental.pallas import tpu as pltpu
from jax.sharding import PartitionSpec as P

MESH = pl.DeviceIdType.MESH
F32 = jnp.float32
BF16 = jnp.bfloat16
TILE = 256
PIECE = 128
STRIP = 128
VMEM_BUDGET = 56 * 1024 * 1024


def halves(x):
    high = x.astype(BF16)
    return high, (x - high.astype(F32)).astype(BF16)


def product(stack, right_high, right_low):
    rows = stack.shape[0] // 2
    both = jnp.dot(stack, right_high, preferred_element_type=F32)
    cross = jnp.dot(stack[:rows], right_low, preferred_element_type=F32)
    return both[:rows] + (both[rows:] + cross)


def look_up(table, index):
    turned = table.T
    high, rest = halves(turned)
    middle = rest
    low = (turned - high.astype(F32) - middle.astype(F32)).astype(BF16)
    shape = (table.shape[0], index.shape[1])
    hot = jnp.where(lax.broadcasted_iota(jnp.int32, shape, 0) == index // 128, 1.0, 0.0).astype(BF16)
    found = jnp.dot(high, hot, preferred_element_type=F32) + (
        jnp.dot(middle, hot, preferred_element_type=F32) + jnp.dot(low, hot, preferred_element_type=F32)
    )
    lane = lax.broadcasted_iota(jnp.int32, found.shape, 0) == lax.rem(index, 128)
    return jnp.sum(jnp.where(lane, found, 0.0), axis=0, keepdims=True)


def kernel(
    na, nb, weight_ref, v_ref, a_ref, alpha_table, beta_table, alpha_index, beta_index, b_hbm, out_ref,
    strip, bt_high, bt_low, v_all, v_col, a_stack, gram, gram_in, scatter, scatter_in,
    square, u_all, total, stack, from_task, to_task, alpha_part, beta_part,
    strip_sem, z_send, z_recv, r_send, g_send, g_recv, e_send, e_recv, s_send, s_recv, x_send, x_recv,
    v_send, v_recv, u_send, u_recv, m_send, m_recv, f_send, f_recv,
):
    a = lax.axis_index("alpha")
    b = lax.axis_index("beta")
    t = lax.axis_index("task")
    rows, cols = v_ref.shape
    full_a = a_ref.shape[1]
    half = cols // 2
    parts = half // PIECE
    quarter = full_a // nb
    eighth = quarter // 2
    across = lax.rem(b + 2, 4)
    sibling = b + 1 - 2 * lax.rem(b, 2)
    diagonal = lax.rem(sibling + 2, 4)
    other = 1 - t
    coef = 0.5 * weight_ref[t]
    inner = lax.rem(a + 1, 4) >= 2

    def peer(d):
        return (a, a + 1 - 2 * lax.rem(a, 2), lax.rem(a + 2, 4), 3 - a)[d]

    barrier = pltpu.get_barrier_semaphore()
    for d in range(1, na):
        pl.semaphore_signal(barrier, inc=1, device_id={"alpha": lax.rem(a + d, na)}, device_id_type=MESH)
    pl.semaphore_signal(barrier, inc=1, device_id={"task": other}, device_id_type=MESH)
    pl.semaphore_signal(barrier, inc=1, device_id={"beta": across}, device_id_type=MESH)
    pl.semaphore_signal(barrier, inc=1, device_id={"beta": sibling}, device_id_type=MESH)
    pl.semaphore_wait(barrier, na + 2)

    def span(start, size):
        return pl.ds(pl.multiple_of(start, 128), size)

    def remote(src, dst, send, recv, where):
        return pltpu.make_async_remote_copy(
            src_ref=src, dst_ref=dst, send_sem=send, recv_sem=recv, device_id=where, device_id_type=MESH
        )

    def piece(side, q):
        return span(side * half + q * PIECE, PIECE)

    def rows_of(i):
        return pl.ds(pl.multiple_of(i * rows, 8), rows)

    def z_copy(q, d):
        return remote(
            v_ref.at[:, piece(t, q)], v_col.at[rows_of(a), piece(t, q)],
            z_send.at[q, d - 1], z_recv.at[q, d - 1], {"alpha": peer(d)},
        )

    def z_relay(q):
        ref = v_col.at[rows_of(peer(2)), piece(t, q)]
        return remote(ref, ref, r_send.at[q], z_recv.at[q, 2], {"alpha": peer(1)})

    def x_copy(q, d):
        at = rows_of(peer(d))
        return remote(
            v_col.at[at, piece(t, q)], v_col.at[at, piece(t, q)],
            x_send.at[q, d - 1], x_recv.at[q, d - 1], {"task": other},
        )

    def g_copy():
        return remote(gram.at[other], gram_in, g_send, g_recv, {"task": other})

    def e_copy(d):
        to = peer(d)
        return remote(scatter.at[rows_of(to), :], scatter_in.at[d - 1], e_send.at[d - 1], e_recv.at[d - 1], {"alpha": to})

    def s_copy():
        ref = square.at[:, span(b * quarter + t * eighth, eighth)]
        return remote(ref, ref, s_send, s_recv, {"task": other})

    def v_copy(n):
        return (
            lambda: remote(v_ref, v_all.at[b], v_send.at[0], v_recv.at[0], {"beta": across}),
            lambda: remote(v_ref, v_all.at[b], v_send.at[1], v_recv.at[1], {"beta": sibling}),
            lambda: remote(v_all.at[across], v_all.at[across], v_send.at[2], v_recv.at[2], {"beta": sibling}),
        )[n]()

    def u_copy(n, k, side, q):
        block = across if n == 2 else b
        ref = u_all.at[block, :, piece(side, q)]
        where = {"beta": across} if n == 0 else {"beta": sibling}
        return remote(ref, ref, u_send.at[n, k], u_recv.at[n, k], where)

    def m_copy(n):
        ref = square.at[:, span((across if n == 2 else b) * quarter, quarter)]
        where = {"beta": across} if n == 0 else {"beta": sibling}
        return remote(ref, ref, m_send.at[n], m_recv.at[n], where)

    def f_copy(q):
        at = pl.ds(q * TILE, TILE)
        return remote(to_task.at[:, at], from_task.at[:, at], f_send.at[q], f_recv.at[q], {"task": other})

    v_copy(0).start()
    v_copy(1).start()
    for q in range(parts):
        z_copy(q, 1).start()
        z_copy(q, 2).start()

        @pl.when(inner)
        def _():
            z_copy(q, 3).start()
    strips = cols // STRIP

    def strip_copy(r, slot):
        return pltpu.make_async_copy(
            b_hbm.at[pl.ds(pl.multiple_of(r * STRIP, STRIP), STRIP), :], strip.at[slot], strip_sem.at[slot]
        )

    strip_copy(0, 0).start()
    v_col[rows_of(a), :] = v_ref[...]
    gram_left, gram_low = halves(a_ref[...].T)
    right_high, right_low = halves(coef * a_ref[:, span(b * quarter, quarter)])
    outer = jnp.dot(gram_left, right_high, preferred_element_type=F32) + (
        jnp.dot(gram_low, right_high, preferred_element_type=F32)
        + jnp.dot(gram_left, right_low, preferred_element_type=F32)
    )
    gram[0] = outer[:, :eighth]
    gram[1] = outer[:, eighth:]
    a_stack[:rows, :], a_stack[rows:, :] = halves(a_ref[...])
    g_copy().start()

    def take_strip(r, carry):
        slot = lax.rem(r, 2)

        @pl.when(r + 1 < strips)
        def _():
            strip_copy(r + 1, 1 - slot).start()

        strip_copy(r, slot).wait()

        def turn(n, inner):
            at = span(n * 512, 512)
            high, low = halves(strip[slot, :, at].T)
            bt_high[at, span(r * STRIP, STRIP)] = high
            bt_low[at, span(r * STRIP, STRIP)] = low
            return inner

        return lax.fori_loop(0, nb * cols // 512, turn, carry)

    lax.fori_loop(0, strips, take_strip, 0)

    def load_block(value):
        stack[:rows, :], stack[rows:, :] = halves(value)

    def add_columns(block, first, start, size):
        def column(n, carry):
            at = span(start + n * TILE, TILE)
            depth = span(block * cols, cols)
            term = product(stack[...], bt_high[depth, at], bt_low[depth, at])
            total[:, at] = term if first else total[:, at] + term
            return carry

        lax.fori_loop(0, size // TILE, column, 0)

    def add_block(value, block, first):
        load_block(value)
        add_columns(block, first, 0, cols)

    def relay_v(q):
        z_copy(q, 2).wait_recv()

        @pl.when(inner)
        def _():
            z_relay(q).start()

        x_copy(q, 2).start()
        for d in (1, 3):
            z_copy(q, d).wait_recv()
            x_copy(q, d).start()

    def make_u(k, side, q):
        at = piece(side, q)
        u_all[b, :, at] = total[:, at] + 2.0 * product(a_stack[...], *halves(v_col[:, at]))
        u_copy(0, k, side, q).start()
        u_copy(1, k, side, q).start()

    add_block(v_ref[...], b, True)
    g_copy().wait_recv()
    scatter[...] = gram[t] + gram_in[...]
    relay_v(0)
    for d in range(1, na):
        e_copy(d).start()
    v_copy(1).wait_recv()
    add_block(v_all[sibling], sibling, False)
    beta_part[...] = look_up(beta_table[...], beta_index[:, span(t * half, half)])
    alpha_row = look_up(alpha_table[...], alpha_index[...])
    alpha_part[...] = jnp.broadcast_to(alpha_row, (128, rows)).T
    relay_v(1)
    v_copy(0).wait_recv()
    v_copy(2).start()
    add_block(v_all[across], across, False)
    v_copy(2).wait_recv()
    add_block(v_all[diagonal], diagonal, False)

    order = []

    def make_next(side, q):
        make_u(len(order), side, q)
        order.append((len(order), side, q))

    for q in range(parts + 1):
        if 2 <= q < parts:
            relay_v(q)
        if q < parts:
            make_next(t, q)
        if q > 0:
            for d in range(1, na):
                x_copy(q - 1, d).wait_recv()
            make_next(other, q - 1)

    def relay_u(pieces):
        for piece_of in pieces:
            u_copy(0, *piece_of).wait_recv()
            u_copy(2, *piece_of).start()

    relay_u(order[:-2])
    add_block(u_all[b], b, True)
    for d in range(1, na):
        e_copy(d).wait_recv()
    mine = scatter[rows_of(a), :]
    for d in range(1, na):
        mine = mine + scatter_in[d - 1]
    square[:, span(b * quarter + t * eighth, eighth)] = mine
    for piece_of in order:
        u_copy(1, *piece_of).wait_recv()
    s_copy().start()
    relay_u(order[-2:])
    load_block(u_all[sibling])
    add_columns(sibling, False, other * half, half)
    s_copy().wait_recv()
    m_copy(0).start()
    m_copy(1).start()
    load_block(u_all[across])
    add_columns(across, False, other * half, half)
    for piece_of in order:
        u_copy(2, *piece_of).wait_recv()
    load_block(u_all[diagonal])
    for q in range(half // TILE):
        at = span(other * half + q * TILE, TILE)
        add_columns(diagonal, False, other * half + q * TILE, TILE)
        to_task[:, q * TILE:(q + 1) * TILE] = coef * total[:, at]
        f_copy(q).start()

    def own_half(n, carry):
        block = lax.rem(b + n, nb)
        load_block(u_all[block])
        add_columns(block, False, t * half, half)
        return carry

    lax.fori_loop(1, nb, own_half, 0)
    m_copy(0).wait_recv()
    m_copy(2).start()
    m_copy(1).wait_recv()
    m_copy(2).wait_recv()
    a_stack[:rows, :], a_stack[rows:, :] = halves(square[...])
    for q in range(half // TILE):
        at = span(t * half + q * TILE, TILE)
        local = pl.ds(q * TILE, TILE)
        diag = alpha_part[:, :1] + beta_part[:, local]
        total[:, at] = (
            coef * total[:, at] + product(a_stack[...], *halves(v_col[:, at])) + diag * v_ref[:, at]
        )
    for q in range(half // TILE):
        f_copy(q).wait_recv()
        local = pl.ds(q * TILE, TILE)
        out_ref[:, local] = total[:, span(t * half + q * TILE, TILE)] + from_task[:, local]

    for q in range(half // TILE):
        f_copy(q).wait_send()
    for q in range(parts):
        z_copy(q, 1).wait_send()
        z_copy(q, 2).wait_send()

        @pl.when(inner)
        def _():
            z_copy(q, 3).wait_send()
            z_relay(q).wait_send()

        for d in range(1, na):
            x_copy(q, d).wait_send()
    g_copy().wait_send()
    s_copy().wait_send()
    for d in range(1, na):
        e_copy(d).wait_send()
    for n in range(3):
        v_copy(n).wait_send()
        m_copy(n).wait_send()
        for piece_of in order:
            u_copy(n, *piece_of).wait_send()


def scratch(na, nb, rows, cols, full_a):
    quarter = full_a // nb
    eighth = quarter // 2
    parts = cols // 2 // PIECE
    buffers = [
        pltpu.VMEM((2, STRIP, nb * cols), F32),
        pltpu.VMEM((nb * cols, cols), BF16),
        pltpu.VMEM((nb * cols, cols), BF16),
        pltpu.VMEM((nb, rows, cols), F32),
        pltpu.VMEM((full_a, cols), F32),
        pltpu.VMEM((2 * rows, full_a), BF16),
        pltpu.VMEM((2, full_a, eighth), F32),
        pltpu.VMEM((full_a, eighth), F32),
        pltpu.VMEM((full_a, eighth), F32),
        pltpu.VMEM((na - 1, rows, eighth), F32),
        pltpu.VMEM((rows, full_a), F32),
        pltpu.VMEM((nb, rows, cols), F32),
        pltpu.VMEM((rows, cols), F32),
        pltpu.VMEM((2 * rows, cols), BF16),
        pltpu.VMEM((rows, cols // 2), F32),
        pltpu.VMEM((rows, cols // 2), F32),
        pltpu.VMEM((rows, 128), F32),
        pltpu.VMEM((1, cols // 2), F32),
    ]
    dma = pltpu.SemaphoreType.DMA
    tiles = cols // 2 // TILE
    counts = [
        (2,), (parts, na - 1), (parts, na - 1), (parts,), (), (), (na - 1,), (na - 1,), (), (), (parts, na - 1), (parts, na - 1),
        (3,), (3,), (3, 2 * parts), (3, 2 * parts), (3,), (3,), (tiles,), (tiles,),
    ]
    return buffers, [dma(c) if c else dma for c in counts]


def fused(
    mesh, op_weight, vector, alpha_rows, beta_rows, alpha_string, beta_string, alpha_energy, beta_energy
):
    na, nb = mesh.shape["alpha"], mesh.shape["beta"]
    rows, cols = vector.shape
    buffers, semaphores = scratch(na, nb, rows, cols, alpha_rows.shape[1])
    vmem = pl.BlockSpec(memory_space=pltpu.VMEM)
    return pl.pallas_call(
        functools.partial(kernel, na, nb),
        out_shape=jax.ShapeDtypeStruct((rows, cols // 2), F32),
        in_specs=[pl.BlockSpec(memory_space=pltpu.SMEM)] + [vmem] * 6 + [pl.BlockSpec(memory_space=pl.ANY)],
        out_specs=vmem,
        scratch_shapes=buffers + semaphores,
        compiler_params=pltpu.CompilerParams(
            collective_id=0, has_side_effects=True, vmem_limit_bytes=60 * 1024 * 1024
        ),
    )(
        op_weight, vector, alpha_rows, alpha_energy.reshape(-1, 128), beta_energy.reshape(-1, 128),
        alpha_string.reshape(1, -1), beta_string.reshape(1, -1), beta_rows,
    )


def fits(mesh, vector, alpha_rows, alpha_energy, beta_energy):
    na, nb, nt = mesh.shape["alpha"], mesh.shape["beta"], mesh.shape["task"]
    rows, cols = vector.shape
    full_a = alpha_rows.shape[1]
    if nb != 4 or nt != 2 or na != 4 or cols % (2 * TILE) or rows % 128 or full_a % (256 * nb):
        return False
    if cols // 2 < 2 * PIECE or alpha_energy.size % 128 or beta_energy.size % 128:
        return False
    buffers, _ = scratch(na, nb, rows, cols, full_a)
    size = sum(buf.dtype.itemsize * functools.reduce(lambda x, y: x * y, buf.shape) for buf in buffers)
    size += 4 * (rows * cols + rows * full_a + rows * cols // 2)
    return size < VMEM_BUDGET


def collective(coefficient, vector, alpha_rows, beta_rows):
    high = lax.Precision.HIGH

    def dot(x, y):
        return jnp.dot(x, y, precision=high, preferred_element_type=F32)

    def apply_operator(block):
        left = dot(alpha_rows, lax.all_gather(block, "alpha", axis=0, tiled=True))
        return left + lax.psum_scatter(dot(block, beta_rows), "beta", scatter_dimension=1, tiled=True)

    second = apply_operator(apply_operator(vector))
    return lax.psum_scatter(coefficient * second, "task", scatter_dimension=1, tiled=True)


def on_device(
    mesh, vector, op_alpha, op_beta, op_weight, alpha_string, beta_string, alpha_energy, beta_energy
):
    if fits(mesh, vector, op_alpha[0], alpha_energy, beta_energy):
        return fused(
            mesh, op_weight, vector, op_alpha[0], op_beta[0],
            alpha_string, beta_string, alpha_energy, beta_energy,
        )
    task_index = lax.axis_index("task")
    summed = collective(0.5 * op_weight[task_index], vector, op_alpha[0], op_beta[0])
    width = summed.shape[1]
    column_start = task_index * width
    own_strings = lax.dynamic_slice_in_dim(beta_string, column_start, width, 0)
    own_vector = lax.dynamic_slice_in_dim(vector, column_start, width, 1)
    diag = alpha_energy[alpha_string][:, None] + beta_energy[own_strings][None, :]
    return summed + diag * own_vector


def solution(mesh):
    return jax.shard_map(
        functools.partial(on_device, mesh),
        mesh=mesh,
        in_specs=(
            P("alpha", "beta"),
            P("task", "alpha", None),
            P("task", "beta", None),
            P(),
            P("alpha"),
            P("beta"),
            P(),
            P(),
        ),
        out_specs=P("alpha", ("beta", "task")),
        check_vma=False,
    )
```

profile of v0, /device:TPU:0, one launch (start us, length us, event | category | flops | bytes accessed | tf_op | source)
XLA Modules:
  0.0 88.4 jit_solution(17337394110257347521)
XLA Ops:
  0.0 86.5 %shard_map.82 = f32[256,512]{1,0:T(8,128)} custom-call(f32[2]{0:T(128)} %weight_ref.1, f32[256,1024]{1,0:T(8,128)} %v_ref.1, f32[256,1024]{1,0:T(8,128)} %bitcast.7, f32[512,128]{1,0:T(8,128)} %bitcast.8, f32[512,128]{1,0:T(8,128)} %bitcast.9, s32[1,256]{1,0:T(1,128)} %bitcast.11, s32[1,1024]{1,0:T(1,128)} %bitcast.10, f32[1024,4096]{1,0:T(8,128)} %bitcast.6), custom_call_target="tpu_custom_call" | custom-call | tf_op jit(solution)/shard_map/pallas_call | solution.py:382
  86.5 1.9 %copy.10 = f32[256,512]{1,0:T(8,128)} copy(f32[256,512]{1,0:T(8,128)} %shard_map.82) | data formatting | bytes 1048576
where the time goes:
time: 88.7 us; the launch traced here: 88.4 us
  Pallas kernels  86.5 us (98%)
  local copies, waits for them, and re-layouts  1.87 us (2%)
    pallas_call x1, Pallas kernels, fused(): pl.pallas_call(functools.partial(kernel, na, nb), out_shape=jax.ShapeDtyp...  86.5 us
    unnamed x1, local copies, waits for them, and re-layouts  1.87 us

commit v1 on v0

v1 whole, which is shorter than its diff:
```python
import functools

import jax
import jax.numpy as jnp
from jax import lax
from jax.experimental import pallas as pl
from jax.experimental.pallas import tpu as pltpu
from jax.sharding import PartitionSpec as P

MESH = pl.DeviceIdType.MESH
F32 = jnp.float32
BF16 = jnp.bfloat16
TILE = 256
STRIP = 128
VMEM_BUDGET = 56 * 1024 * 1024


TURNED = (((1,), (1,)), ((), ()))


def pieces_of(half):
    return [(0, half // 2), (half // 2, half // 4), (half // 2 + half // 4, half // 4)]


def block_span(i, size):
    return pl.ds(pl.multiple_of(i * size, 128), size)


def halves(x):
    high = x.astype(BF16)
    return high, (x - high.astype(F32)).astype(BF16)


def product(stack, right_high, right_low):
    rows = stack.shape[0] // 2
    both = jnp.dot(stack, right_high, preferred_element_type=F32)
    cross = jnp.dot(stack[:rows], right_low, preferred_element_type=F32)
    return both[:rows] + (both[rows:] + cross)


def look_up(table, index):
    turned = table.T
    high, rest = halves(turned)
    middle = rest
    low = (turned - high.astype(F32) - middle.astype(F32)).astype(BF16)
    shape = (table.shape[0], index.shape[1])
    hot = jnp.where(lax.broadcasted_iota(jnp.int32, shape, 0) == index // 128, 1.0, 0.0).astype(BF16)
    found = jnp.dot(high, hot, preferred_element_type=F32) + (
        jnp.dot(middle, hot, preferred_element_type=F32) + jnp.dot(low, hot, preferred_element_type=F32)
    )
    lane = lax.broadcasted_iota(jnp.int32, found.shape, 0) == lax.rem(index, 128)
    return jnp.sum(jnp.where(lane, found, 0.0), axis=0, keepdims=True)


def kernel(
    na, nb, weight_ref, v_ref, a_ref, alpha_table, beta_table, alpha_index, beta_index, b_hbm, out_ref,
    strip, b_high, b_low, v_all, v_col, a_other, a_stack, stack, total, acc, p_own, ret_out, ret_in, u_all,
    gram, gram_end, sum_out, sum_in, last_out, last_in, square, square_stack, from_task, to_task,
    alpha_part, beta_part,
    strip_sem, z_send, z_recv, r_send, a_send, a_recv, p_send, p_recv,
    e_send, e_recv, s_send, s_recv, v_send, v_recv, k_send, k_recv, u_send, u_recv, m_send, m_recv, f_send, f_recv,
):
    a = lax.axis_index("alpha")
    b = lax.axis_index("beta")
    t = lax.axis_index("task")
    rows, cols = v_ref.shape
    full_a = a_ref.shape[1]
    half = cols // 2
    slab = cols // 4
    quarter = full_a // nb
    eighth = quarter // 2
    across = lax.rem(b + 2, 4)
    core = lax.rem(b, 2)
    sibling = b + 1 - 2 * core
    diagonal = lax.rem(sibling + 2, 4)
    other = 1 - t
    coef = 0.5 * weight_ref[t]
    coef_other = 0.5 * weight_ref[other]
    inner = lax.rem(a + 1, 4) >= 2
    outer = lax.rem(a + 1, 4) < 2
    pieces = pieces_of(half)
    steps = range(len(pieces))

    def peer(d):
        return (a, a + 1 - 2 * lax.rem(a, 2), lax.rem(a + 2, 4), 3 - a)[d]

    def span(start, size):
        return pl.ds(pl.multiple_of(start, 128), size)

    def remote(src, dst, send, recv, where):
        return pltpu.make_async_remote_copy(
            src_ref=src, dst_ref=dst, send_sem=send, recv_sem=recv, device_id=where, device_id_type=MESH
        )

    def rows_of(i):
        return pl.ds(pl.multiple_of(i * rows, 8), rows)

    def local(q):
        return pl.ds(*pieces[q])

    def piece(side, q):
        return span(side * half + pieces[q][0], pieces[q][1])

    def z_copy(q, d):
        return remote(
            v_ref.at[:, piece(t, q)], v_col.at[rows_of(a), local(q)],
            z_send.at[q, d - 1], z_recv.at[q, d - 1], {"alpha": peer(d)},
        )

    def z_relay(q, d):
        ref = v_col.at[rows_of(peer(d)), local(q)]
        return remote(ref, ref, r_send.at[q, d - 2], z_recv.at[q, 4 - d], {"alpha": peer(1)})

    def a_copy():
        at = pl.ds(pl.multiple_of(core * (rows // 2), 8), rows // 2)
        return remote(a_ref.at[at, :], a_other.at[at, :], a_send.at[0], a_recv.at[0], {"task": other})

    def a_relay():
        at = pl.ds(pl.multiple_of(core * (rows // 2), 8), rows // 2)
        return remote(a_other.at[at, :], a_other.at[at, :], a_send.at[1], a_recv.at[1], {"beta": sibling})

    def slab_of(n):
        return (2 + t, 0, 1, 2 + other)[n]

    def v_copy(n):
        at = span(slab_of(n) * slab, slab)
        return remote(v_ref.at[:, at], v_all.at[b, :, at], v_send.at[n], v_recv.at[n], {"beta": across})

    def v_pass():
        ref = v_all.at[across, :, span((2 + t) * slab, slab)]
        return remote(ref, ref, v_send.at[3], v_recv.at[3], {"task": other})

    def v_near():
        return remote(v_ref, v_all.at[b], k_send.at[4], k_recv.at[4], {"beta": sibling})

    def v_relay(n):
        ref = v_all.at[across, :, span(slab_of(n) * slab, slab)]
        return remote(ref, ref, k_send.at[n], k_recv.at[n], {"beta": sibling})

    def v_relayed(n):
        ref = v_all.at[diagonal, :, span(slab_of(n) * slab, slab)]
        return remote(ref, ref, k_send.at[n], k_recv.at[n], {"beta": sibling})

    def p_copy(q):
        at = local(q)
        return remote(ret_out.at[:, at], ret_in.at[:, at], p_send.at[q], p_recv.at[q], {"task": other})

    def u_copy(n, k, side, q):
        block = across if n == 2 else b
        ref = u_all.at[block, :, piece(side, q)]
        where = {"beta": across} if n == 0 else {"beta": sibling}
        return remote(ref, ref, u_send.at[n, k], u_recv.at[n, k], where)

    far = span(rows * jnp.where(a == 0, 1, 0), (na - 1) * rows)
    far_pair = span(rows * jnp.where(a < 2, 2, 0), 2 * rows)

    def e_copy(n):
        if n == 0:
            return remote(gram.at[:, far], gram_end.at[:, far], e_send.at[0], e_recv.at[0], {"alpha": peer(1)})
        if n == 1:
            return remote(sum_out, sum_in, e_send.at[1], e_recv.at[1], {"alpha": peer(3)})
        return remote(last_out, last_in, e_send.at[2], e_recv.at[2], {"alpha": peer(1)})

    def s_copy():
        ref = square.at[:, span(b * quarter + t * eighth, eighth)]
        return remote(ref, ref, s_send, s_recv, {"task": other})

    def m_copy(n):
        ref = square.at[:, span((across if n == 2 else b) * quarter, quarter)]
        where = {"beta": across} if n == 0 else {"beta": sibling}
        return remote(ref, ref, m_send.at[n], m_recv.at[n], where)

    def f_copy(q):
        at = pl.ds(q * TILE, TILE)
        return remote(to_task.at[:, at], from_task.at[:, at], f_send.at[q], f_recv.at[q], {"task": other})

    strips = cols // STRIP

    def strip_copy(r, slot):
        return pltpu.make_async_copy(
            b_hbm.at[pl.ds(pl.multiple_of(r * STRIP, STRIP), STRIP), :], strip.at[slot], strip_sem.at[slot]
        )

    barrier = pltpu.get_barrier_semaphore()
    for d in range(1, na):
        pl.semaphore_signal(barrier, inc=1, device_id={"alpha": lax.rem(a + d, na)}, device_id_type=MESH)
    pl.semaphore_signal(barrier, inc=1, device_id={"task": other}, device_id_type=MESH)
    pl.semaphore_signal(barrier, inc=1, device_id={"beta": across}, device_id_type=MESH)
    pl.semaphore_signal(barrier, inc=1, device_id={"beta": sibling}, device_id_type=MESH)
    strip_copy(0, 0).start()
    strip_copy(1, 1).start()
    pl.semaphore_wait(barrier, na + 2)

    v_copy(0).start()
    a_copy().start()
    for q in steps:
        z_copy(q, 1).start()

        @pl.when(outer)
        def _():
            z_copy(q, 2).start()

        @pl.when(inner)
        def _():
            z_copy(q, 3).start()

    v_copy(1).start()
    v_copy(2).start()
    v_near().start()

    def take_strip(r, carry):
        slot = lax.rem(r, 2)
        strip_copy(r, slot).wait()
        at = pl.ds(pl.multiple_of(r * STRIP, STRIP), STRIP)

        def turn(n, inside):
            wide = span(n * 512, 512)
            b_high[at, wide], b_low[at, wide] = halves(strip[slot, :, wide])
            return inside

        lax.fori_loop(0, nb * cols // 512, turn, carry)

        @pl.when(r + 2 < strips)
        def _():
            strip_copy(r + 2, slot).start()

        return carry

    lax.fori_loop(0, strips, take_strip, 0)

    def multiply(lhs, rhs_high, rhs_low):
        n = lhs.shape[0] // 2
        both = lax.dot_general(lhs, rhs_high, TURNED, preferred_element_type=F32)
        cross = lax.dot_general(lhs[:n], rhs_low, TURNED, preferred_element_type=F32)
        return both[:n] + (both[n:] + cross)

    def accumulate(into, value, block, parts, start, size, first=False):
        for at in parts:
            stack[:rows, at], stack[rows:, at] = halves(value[:, at])

        def joined(ref, at_rows, shift):
            found = [ref[at_rows, pl.ds(pl.multiple_of(shift + at.start, 128), at.size)] for at in parts]
            return found[0] if len(found) == 1 else jnp.concatenate(found, axis=1)

        at = span(start, size)
        term = multiply(joined(stack, slice(None), 0), joined(b_high, at, block * cols), joined(b_low, at, block * cols))
        into[:, at] = term if first else into[:, at] + term

    whole = [pl.ds(0, cols)]

    def relay_z(q):
        @pl.when(inner)
        def _():
            for d in (3, 2):
                z_copy(q, d).wait_recv()
                z_relay(q, d).start()

    def project(q):
        z_copy(q, 1).wait_recv()

        @pl.when(outer)
        def _():
            for d in (2, 3):
                z_copy(q, d).wait_recv()

        both = 2.0 * product(a_stack[...], *halves(v_col[:, local(q)]))
        ret_out[:, local(q)] = both[rows:]
        p_copy(q).start()
        p_own[:, local(q)] = both[:rows]

    order = []

    def make_u(side, q):
        if side is other:
            p_copy(q).wait_recv()
        at = piece(side, q)
        u_all[b, :, at] = total[:, at] + (ret_in if side is other else p_own)[:, local(q)]
        k = len(order)
        order.append((k, side, q))
        u_copy(0, k, side, q).start()
        u_copy(1, k, side, q).start()

    def u_parts(q0, q1):
        start = pieces[q0][0]
        size = pieces[q1][0] + pieces[q1][1] - start
        return [pl.ds(start, size), pl.ds(half + start, size)]

    accumulate(total, v_ref, b, whole, 0, cols, True)
    v_copy(0).wait_recv()
    v_pass().start()
    v_relay(0).start()
    relay_z(0)
    v_near().wait_recv()
    accumulate(total, v_all.at[sibling], sibling, whole, 0, cols)
    a_copy().wait_recv()
    a_relay().start()
    v_copy(1).wait_recv()
    v_relay(1).start()
    own_high, own_low = halves(a_ref[...])
    a_stack[:rows, :] = own_high
    a_stack[2 * rows:3 * rows, :] = own_low
    v_col[rows_of(a), :] = v_ref[:, span(t * half, half)]
    beta_part[...] = look_up(beta_table[...], beta_index[:, span(t * half, half)])
    a_relay().wait_recv()
    other_high, other_low = halves(a_other[...])
    a_stack[rows:2 * rows, :] = other_high
    a_stack[3 * rows:, :] = other_low
    at = span(b * quarter + t * eighth, eighth)
    left = jnp.concatenate([(coef * a_ref[:, at]).T, (coef_other * a_other[:, at]).T], axis=1)
    left_high, left_low = halves(left)
    a_high, a_low = a_stack[:2 * rows, :], a_stack[2 * rows:, :]
    gram[...] = jnp.dot(left_high, a_high, preferred_element_type=F32) + (
        jnp.dot(left_low, a_high, preferred_element_type=F32) + jnp.dot(left_high, a_low, preferred_element_type=F32)
    )

    @pl.when(outer)
    def _():
        e_copy(0).start()

    project(0)
    relay_z(1)
    v_copy(2).wait_recv()
    v_relay(2).start()
    v_pass().wait_recv()
    v_relay(3).start()
    accumulate(total, v_all.at[across], across, whole, 0, cols)
    for n in range(4):
        v_relayed(n).wait_recv()
    accumulate(total, v_all.at[diagonal], diagonal, whole, 0, cols)

    def relay_u(k):
        u_copy(0, *order[k]).wait_recv()
        u_copy(2, *order[k]).start()

    make_u(t, 0)
    make_u(other, 0)
    relay_z(2)
    accumulate(acc, u_all.at[b], b, u_parts(0, 0), 0, cols, True)
    u_copy(1, *order[0]).wait_recv()
    u_copy(1, *order[1]).wait_recv()
    accumulate(acc, u_all.at[sibling], sibling, u_parts(0, 0), 0, cols)

    @pl.when(inner)
    def _():
        e_copy(0).wait_recv()
        sum_out[...] = gram[:, far_pair] + gram_end[:, far_pair]
        e_copy(1).start()

    project(1)
    make_u(t, 1)
    relay_u(0)
    make_u(other, 1)
    alpha_row = look_up(alpha_table[...], alpha_index[...])
    alpha_part[...] = jnp.broadcast_to(alpha_row, (128, rows)).T

    @pl.when(inner)
    def _():
        e_copy(1).wait_recv()
        last_out[...] = gram[:, block_span(peer(1), rows)] + sum_in[:, block_span(a - 1, rows)]
        e_copy(2).start()
        kept = gram[:, block_span(a, rows)] + (gram_end[:, block_span(a, rows)] + sum_in[:, block_span(2 - a, rows)])
        square[:, span(b * quarter + t * eighth, eighth)] = kept.T

    relay_u(1)
    accumulate(acc, u_all.at[across], across, u_parts(0, 0), 0, cols)
    project(2)
    make_u(t, 2)
    u_copy(2, *order[0]).wait_recv()
    u_copy(2, *order[1]).wait_recv()
    accumulate(acc, u_all.at[diagonal], diagonal, u_parts(0, 0), 0, cols)
    relay_u(2)
    make_u(other, 2)

    @pl.when(outer)
    def _():
        e_copy(2).wait_recv()
        square[:, span(b * quarter + t * eighth, eighth)] = (gram[:, block_span(a, rows)] + last_in[...]).T

    s_copy().start()
    relay_u(3)
    accumulate(acc, u_all.at[b], b, u_parts(1, 2), 0, cols)
    for k in range(2, len(order)):
        u_copy(1, *order[k]).wait_recv()
    accumulate(acc, u_all.at[sibling], sibling, u_parts(1, 2), 0, cols)
    relay_u(4)
    s_copy().wait_recv()
    m_copy(0).start()
    m_copy(1).start()
    relay_u(5)
    accumulate(acc, u_all.at[across], across, u_parts(1, 2), other * half, half)
    for k in range(2, len(order)):
        u_copy(2, *order[k]).wait_recv()
    for q in range(half // TILE):
        at = span(other * half + q * TILE, TILE)
        accumulate(acc, u_all.at[diagonal], diagonal, u_parts(1, 2), other * half + q * TILE, TILE)
        to_task[:, q * TILE:(q + 1) * TILE] = coef * acc[:, at]
        f_copy(q).start()
    accumulate(acc, u_all.at[across], across, u_parts(1, 2), t * half, half)
    accumulate(acc, u_all.at[diagonal], diagonal, u_parts(1, 2), t * half, half)
    m_copy(0).wait_recv()
    m_copy(2).start()
    m_copy(1).wait_recv()
    m_copy(2).wait_recv()
    square_stack[:rows, :], square_stack[rows:, :] = halves(square[...])
    for q in range(half // TILE):
        at = span(t * half + q * TILE, TILE)
        within = pl.ds(q * TILE, TILE)
        diag = alpha_part[:, :1] + beta_part[:, within]
        acc[:, at] = coef * acc[:, at] + product(square_stack[...], *halves(v_col[:, within])) + diag * v_ref[:, at]
    for q in range(half // TILE):
        f_copy(q).wait_recv()
        within = pl.ds(q * TILE, TILE)
        out_ref[:, within] = acc[:, span(t * half + q * TILE, TILE)] + from_task[:, within]

    for q in range(half // TILE):
        f_copy(q).wait_send()
    for q in steps:
        z_copy(q, 1).wait_send()
        p_copy(q).wait_send()

        @pl.when(outer)
        def _():
            z_copy(q, 2).wait_send()

        @pl.when(inner)
        def _():
            z_copy(q, 3).wait_send()
            z_relay(q, 2).wait_send()
            z_relay(q, 3).wait_send()

    @pl.when(outer)
    def _():
        e_copy(0).wait_send()

    @pl.when(inner)
    def _():
        e_copy(1).wait_send()
        e_copy(2).wait_send()

    a_copy().wait_send()
    a_relay().wait_send()
    for n in range(3):
        v_copy(n).wait_send()
        m_copy(n).wait_send()
        for piece_of in order:
            u_copy(n, *piece_of).wait_send()
    v_pass().wait_send()
    v_near().wait_send()
    for n in range(4):
        v_relay(n).wait_send()
    s_copy().wait_send()


def scratch(na, nb, rows, cols, full_a):
    quarter = full_a // nb
    eighth = quarter // 2
    half = cols // 2
    buffers = [
        pltpu.VMEM((2, STRIP, nb * cols), F32),
        pltpu.VMEM((cols, nb * cols), BF16),
        pltpu.VMEM((cols, nb * cols), BF16),
        pltpu.VMEM((nb, rows, cols), F32),
        pltpu.VMEM((full_a, half), F32),
        pltpu.VMEM((rows, full_a), F32),
        pltpu.VMEM((4 * rows, full_a), BF16),
        pltpu.VMEM((2 * rows, cols), BF16),
        pltpu.VMEM((rows, cols), F32),
        pltpu.VMEM((rows, cols), F32),
        pltpu.VMEM((rows, half), F32),
        pltpu.VMEM((rows, half), F32),
        pltpu.VMEM((rows, half), F32),
        pltpu.VMEM((nb, rows, cols), F32),
        pltpu.VMEM((eighth, full_a), F32),
        pltpu.VMEM((eighth, full_a), F32),
        pltpu.VMEM((eighth, 2 * rows), F32),
        pltpu.VMEM((eighth, 2 * rows), F32),
        pltpu.VMEM((eighth, rows), F32),
        pltpu.VMEM((eighth, rows), F32),
        pltpu.VMEM((rows, full_a), F32),
        pltpu.VMEM((2 * rows, full_a), BF16),
        pltpu.VMEM((rows, half), F32),
        pltpu.VMEM((rows, half), F32),
        pltpu.VMEM((rows, 128), F32),
        pltpu.VMEM((1, half), F32),
    ]
    dma = pltpu.SemaphoreType.DMA
    tiles = half // TILE
    parts = len(pieces_of(half))
    counts = [
        (2,), (parts, 3), (parts, 3), (parts, 2), (2,), (2,), (parts,), (parts,),
        (3,), (3,), (), (), (4,), (4,), (5,), (5,), (3, 2 * parts), (3, 2 * parts), (3,), (3,), (tiles,), (tiles,),
    ]
    return buffers, [dma(c) if c else dma for c in counts]


def fused(
    mesh, op_weight, vector, alpha_rows, beta_rows, alpha_string, beta_string, alpha_energy, beta_energy
):
    na, nb = mesh.shape["alpha"], mesh.shape["beta"]
    rows, cols = vector.shape
    buffers, semaphores = scratch(na, nb, rows, cols, alpha_rows.shape[1])
    vmem = pl.BlockSpec(memory_space=pltpu.VMEM)
    return pl.pallas_call(
        functools.partial(kernel, na, nb),
        out_shape=jax.ShapeDtypeStruct((rows, cols // 2), F32),
        in_specs=[pl.BlockSpec(memory_space=pltpu.SMEM)] + [vmem] * 6 + [pl.BlockSpec(memory_space=pl.ANY)],
        out_specs=vmem,
        scratch_shapes=buffers + semaphores,
        compiler_params=pltpu.CompilerParams(
            collective_id=0, has_side_effects=True, vmem_limit_bytes=60 * 1024 * 1024
        ),
    )(
        op_weight, vector, alpha_rows, alpha_energy.reshape(-1, 128), beta_energy.reshape(-1, 128),
        alpha_string.reshape(1, -1), beta_string.reshape(1, -1), beta_rows,
    )


def fits(mesh, vector, alpha_rows, alpha_energy, beta_energy):
    na, nb, nt = mesh.shape["alpha"], mesh.shape["beta"], mesh.shape["task"]
    rows, cols = vector.shape
    full_a = alpha_rows.shape[1]
    if nb != 4 or nt != 2 or na != 4 or cols % (8 * 128) or rows % 128 or full_a % (256 * nb) or full_a != na * rows:
        return False
    if alpha_energy.size % 128 or beta_energy.size % 128:
        return False
    buffers, _ = scratch(na, nb, rows, cols, full_a)
    size = sum(buf.dtype.itemsize * functools.reduce(lambda x, y: x * y, buf.shape) for buf in buffers)
    size += 4 * (rows * cols + rows * full_a + rows * cols // 2)
    return size < VMEM_BUDGET


def collective(coefficient, vector, alpha_rows, beta_rows):
    high = lax.Precision.HIGH

    def dot(x, y):
        return jnp.dot(x, y, precision=high, preferred_element_type=F32)

    def apply_operator(block):
        left = dot(alpha_rows, lax.all_gather(block, "alpha", axis=0, tiled=True))
        return left + lax.psum_scatter(dot(block, beta_rows), "beta", scatter_dimension=1, tiled=True)

    second = apply_operator(apply_operator(vector))
    return lax.psum_scatter(coefficient * second, "task", scatter_dimension=1, tiled=True)


def on_device(
    mesh, vector, op_alpha, op_beta, op_weight, alpha_string, beta_string, alpha_energy, beta_energy
):
    if fits(mesh, vector, op_alpha[0], alpha_energy, beta_energy):
        return fused(
            mesh, op_weight, vector, op_alpha[0], op_beta[0],
            alpha_string, beta_string, alpha_energy, beta_energy,
        )
    task_index = lax.axis_index("task")
    summed = collective(0.5 * op_weight[task_index], vector, op_alpha[0], op_beta[0])
    width = summed.shape[1]
    column_start = task_index * width
    own_strings = lax.dynamic_slice_in_dim(beta_string, column_start, width, 0)
    own_vector = lax.dynamic_slice_in_dim(vector, column_start, width, 1)
    diag = alpha_energy[alpha_string][:, None] + beta_energy[own_strings][None, :]
    return summed + diag * own_vector


def solution(mesh):
    return jax.shard_map(
        functools.partial(on_device, mesh),
        mesh=mesh,
        in_specs=(
            P("alpha", "beta"),
            P("task", "alpha", None),
            P("task", "beta", None),
            P(),
            P("alpha"),
            P("beta"),
            P(),
            P(),
        ),
        out_specs=P("alpha", ("beta", "task")),
        check_vma=False,
    )
```

time: 88.7 us -> 84.6 us (0.954)
  Pallas kernels: 86.5 us -> 82.5 us
    pallas_call x1, Pallas kernels: 86.5 us -> 82.5 us  [fused(): pl.pallas_call(functools.partial(kernel, na, nb), out_shape=jax.ShapeDtyp...]
where the time goes in v1:
time: 84.6 us; the launch traced here: 84.3 us
  Pallas kernels  82.5 us (98%)
  local copies, waits for them, and re-layouts  1.87 us (2%)
    pallas_call x1, Pallas kernels, fused(): pl.pallas_call(functools.partial(kernel, na, nb), out_shape=jax.ShapeDtyp...  82.5 us
    unnamed x1, local copies, waits for them, and re-layouts  1.87 us

profile of v1, /device:TPU:0, one launch (start us, length us, event | category | flops | bytes accessed | tf_op | source)
XLA Modules:
  0.0 84.3 jit_solution(10484317414587183995)
XLA Ops:
  0.0 82.5 %shard_map.82 = f32[256,512]{1,0:T(8,128)} custom-call(f32[2]{0:T(128)} %weight_ref.1, f32[256,1024]{1,0:T(8,128)} %v_ref.1, f32[256,1024]{1,0:T(8,128)} %bitcast.7, f32[512,128]{1,0:T(8,128)} %bitcast.8, f32[512,128]{1,0:T(8,128)} %bitcast.9, s32[1,256]{1,0:T(1,128)} %bitcast.11, s32[1,1024]{1,0:T(1,128)} %bitcast.10, f32[1024,4096]{1,0:T(8,128)} %bitcast.6), custom_call_target="tpu_custom_call" | custom-call | tf_op jit(solution)/shard_map/pallas_call | solution.py:503
  82.5 1.9 %copy.10 = f32[256,512]{1,0:T(8,128)} copy(f32[256,512]{1,0:T(8,128)} %shard_map.82) | data formatting | bytes 1048576

commit v2 on v1

--- a/solution.py
+++ b/solution.py
@@ -19,7 +19,7 @@
 
 
 def pieces_of(half):
-    return [(0, half // 2), (half // 2, half // 4), (half // 2 + half // 4, half // 4)]
+    return [(n * (half // 4), half // 4) for n in range(4)]
 
 
 def block_span(i, size):
@@ -53,18 +53,18 @@
 
 
 def kernel(
-    na, nb, weight_ref, v_ref, a_ref, alpha_table, beta_table, alpha_index, beta_index, b_hbm, out_ref,
-    strip, b_high, b_low, v_all, v_col, a_other, a_stack, stack, total, acc, p_own, ret_out, ret_in, u_all,
+    na, nb, weight_ref, v_hbm, a_hbm, alpha_hbm, beta_hbm, alpha_index, beta_index, b_hbm, out_ref,
+    a_ref, alpha_table, beta_table, strip, b_high, b_low, v_all, v_col, a_other, a_stack, stack, total, acc, p_own, ret_out, ret_in, u_all,
     gram, gram_end, sum_out, sum_in, last_out, last_in, square, square_stack, from_task, to_task,
     alpha_part, beta_part,
-    strip_sem, z_send, z_recv, r_send, a_send, a_recv, p_send, p_recv,
+    local_sem, strip_sem, z_send, z_recv, r_send, a_send, a_recv, p_send, p_recv,
     e_send, e_recv, s_send, s_recv, v_send, v_recv, k_send, k_recv, u_send, u_recv, m_send, m_recv, f_send, f_recv,
 ):
     a = lax.axis_index("alpha")
     b = lax.axis_index("beta")
     t = lax.axis_index("task")
-    rows, cols = v_ref.shape
-    full_a = a_ref.shape[1]
+    rows, cols = v_hbm.shape
+    full_a = a_hbm.shape[1]
     half = cols // 2
     slab = cols // 4
     quarter = full_a // nb
@@ -103,7 +103,7 @@
 
     def z_copy(q, d):
         return remote(
-            v_ref.at[:, piece(t, q)], v_col.at[rows_of(a), local(q)],
+            v_hbm.at[:, piece(t, q)], v_col.at[rows_of(a), local(q)],
             z_send.at[q, d - 1], z_recv.at[q, d - 1], {"alpha": peer(d)},
         )
 
@@ -113,7 +113,7 @@
 
     def a_copy():
         at = pl.ds(pl.multiple_of(core * (rows // 2), 8), rows // 2)
-        return remote(a_ref.at[at, :], a_other.at[at, :], a_send.at[0], a_recv.at[0], {"task": other})
+        return remote(a_hbm.at[at, :], a_other.at[at, :], a_send.at[0], a_recv.at[0], {"task": other})
 
     def a_relay():
         at = pl.ds(pl.multiple_of(core * (rows // 2), 8), rows // 2)
@@ -122,16 +122,19 @@
     def slab_of(n):
         return (2 + t, 0, 1, 2 + other)[n]
 
+    def slab_span(n):
+        return span(slab_of(n) * slab, slab)
+
     def v_copy(n):
         at = span(slab_of(n) * slab, slab)
-        return remote(v_ref.at[:, at], v_all.at[b, :, at], v_send.at[n], v_recv.at[n], {"beta": across})
+        return remote(v_hbm.at[:, at], v_all.at[b, :, at], v_send.at[n], v_recv.at[n], {"beta": across})
 
     def v_pass():
         ref = v_all.at[across, :, span((2 + t) * slab, slab)]
         return remote(ref, ref, v_send.at[3], v_recv.at[3], {"task": other})
 
     def v_near():
-        return remote(v_ref, v_all.at[b], k_send.at[4], k_recv.at[4], {"beta": sibling})
+        return remote(v_hbm, v_all.at[b], k_send.at[4], k_recv.at[4], {"beta": sibling})
 
     def v_relay(n):
         ref = v_all.at[across, :, span(slab_of(n) * slab, slab)]
@@ -180,6 +183,10 @@
         return pltpu.make_async_copy(
             b_hbm.at[pl.ds(pl.multiple_of(r * STRIP, STRIP), STRIP), :], strip.at[slot], strip_sem.at[slot]
         )
+
+    def stage(n):
+        source = (v_hbm, a_hbm, beta_hbm, alpha_hbm)[n]
+        return pltpu.make_async_copy(source, (v_all.at[b], a_ref, beta_table, alpha_table)[n], local_sem.at[n])
 
     barrier = pltpu.get_barrier_semaphore()
     for d in range(1, na):
@@ -189,20 +196,24 @@
     pl.semaphore_signal(barrier, inc=1, device_id={"beta": sibling}, device_id_type=MESH)
     strip_copy(0, 0).start()
     strip_copy(1, 1).start()
+    for n in range(4):
+        stage(n).start()
     pl.semaphore_wait(barrier, na + 2)
 
     v_copy(0).start()
     a_copy().start()
-    for q in steps:
-        z_copy(q, 1).start()
-
-        @pl.when(outer)
-        def _():
+
+    @pl.when(outer)
+    def _():
+        for q in steps:
             z_copy(q, 2).start()
-
-        @pl.when(inner)
-        def _():
+            z_copy(q, 1).start()
+
+    @pl.when(inner)
+    def _():
+        for q in steps:
             z_copy(q, 3).start()
+            z_copy(q, 1).start()
 
     v_copy(1).start()
     v_copy(2).start()
@@ -285,26 +296,34 @@
         size = pieces[q1][0] + pieces[q1][1] - start
         return [pl.ds(start, size), pl.ds(half + start, size)]
 
-    accumulate(total, v_ref, b, whole, 0, cols, True)
     v_copy(0).wait_recv()
     v_pass().start()
     v_relay(0).start()
+    for n in range(4):
+        stage(n).wait()
+    accumulate(total, v_all.at[b], b, whole, 0, cols, True)
     relay_z(0)
+    own_high, own_low = halves(a_ref[...])
+    a_stack[:rows, :] = own_high
+    a_stack[2 * rows:3 * rows, :] = own_low
+    v_col[rows_of(a), :] = v_all[b, :, span(t * half, half)]
     v_near().wait_recv()
     accumulate(total, v_all.at[sibling], sibling, whole, 0, cols)
+    relay_z(1)
     a_copy().wait_recv()
     a_relay().start()
     v_copy(1).wait_recv()
     v_relay(1).start()
-    own_high, own_low = halves(a_ref[...])
-    a_stack[:rows, :] = own_high
-    a_stack[2 * rows:3 * rows, :] = own_low
-    v_col[rows_of(a), :] = v_ref[:, span(t * half, half)]
-    beta_part[...] = look_up(beta_table[...], beta_index[:, span(t * half, half)])
+    early = [slab_span(n) for n in (0, 1)]
+    late = [slab_span(n) for n in (2, 3)]
+    accumulate(total, v_all.at[across], across, early, 0, cols)
     a_relay().wait_recv()
     other_high, other_low = halves(a_other[...])
     a_stack[rows:2 * rows, :] = other_high
     a_stack[3 * rows:, :] = other_low
+    for n in range(2):
+        v_relayed(n).wait_recv()
+    accumulate(total, v_all.at[diagonal], diagonal, early, 0, cols)
     at = span(b * quarter + t * eighth, eighth)
     left = jnp.concatenate([(coef * a_ref[:, at]).T, (coef_other * a_other[:, at]).T], axis=1)
     left_high, left_low = halves(left)
@@ -317,28 +336,37 @@
     def _():
         e_copy(0).start()
 
-    project(0)
-    relay_z(1)
     v_copy(2).wait_recv()
     v_relay(2).start()
     v_pass().wait_recv()
     v_relay(3).start()
-    accumulate(total, v_all.at[across], across, whole, 0, cols)
-    for n in range(4):
+    relay_z(2)
+    project(0)
+    accumulate(total, v_all.at[across], across, late, 0, cols)
+    for n in range(2, 4):
         v_relayed(n).wait_recv()
-    accumulate(total, v_all.at[diagonal], diagonal, whole, 0, cols)
+    accumulate(total, v_all.at[diagonal], diagonal, late, 0, cols)
 
     def relay_u(k):
         u_copy(0, *order[k]).wait_recv()
         u_copy(2, *order[k]).start()
 
     make_u(t, 0)
+    relay_z(3)
     make_u(other, 0)
-    relay_z(2)
-    accumulate(acc, u_all.at[b], b, u_parts(0, 0), 0, cols, True)
-    u_copy(1, *order[0]).wait_recv()
-    u_copy(1, *order[1]).wait_recv()
-    accumulate(acc, u_all.at[sibling], sibling, u_parts(0, 0), 0, cols)
+    project(1)
+    make_u(t, 1)
+    relay_u(0)
+    beta_part[...] = look_up(beta_table[...], beta_index[:, span(t * half, half)])
+    relay_u(1)
+    make_u(other, 1)
+    accumulate(acc, u_all.at[b], b, u_parts(0, 1), 0, cols, True)
+    project(2)
+    make_u(t, 2)
+    for k in range(4):
+        u_copy(1, *order[k]).wait_recv()
+    accumulate(acc, u_all.at[sibling], sibling, u_parts(0, 1), 0, cols)
+    relay_u(2)
 
     @pl.when(inner)
     def _():
@@ -346,12 +374,12 @@
         sum_out[...] = gram[:, far_pair] + gram_end[:, far_pair]
         e_copy(1).start()
 
-    project(1)
-    make_u(t, 1)
-    relay_u(0)
-    make_u(other, 1)
-    alpha_row = look_up(alpha_table[...], alpha_index[...])
-    alpha_part[...] = jnp.broadcast_to(alpha_row, (128, rows)).T
+    relay_u(3)
+    make_u(other, 2)
+    project(3)
+    make_u(t, 3)
+    accumulate(acc, u_all.at[across], across, u_parts(0, 1), 0, cols)
+    relay_u(4)
 
     @pl.when(inner)
     def _():
@@ -361,15 +389,11 @@
         kept = gram[:, block_span(a, rows)] + (gram_end[:, block_span(a, rows)] + sum_in[:, block_span(2 - a, rows)])
         square[:, span(b * quarter + t * eighth, eighth)] = kept.T
 
-    relay_u(1)
-    accumulate(acc, u_all.at[across], across, u_parts(0, 0), 0, cols)
-    project(2)
-    make_u(t, 2)
-    u_copy(2, *order[0]).wait_recv()
-    u_copy(2, *order[1]).wait_recv()
-    accumulate(acc, u_all.at[diagonal], diagonal, u_parts(0, 0), 0, cols)
-    relay_u(2)
-    make_u(other, 2)
+    for k in range(4):
+        u_copy(2, *order[k]).wait_recv()
+    accumulate(acc, u_all.at[diagonal], diagonal, u_parts(0, 1), 0, cols)
+    make_u(other, 3)
+    relay_u(5)
 
     @pl.when(outer)
     def _():
@@ -377,26 +401,32 @@
         square[:, span(b * quarter + t * eighth, eighth)] = (gram[:, block_span(a, rows)] + last_in[...]).T
 
     s_copy().start()
-    relay_u(3)
-    accumulate(acc, u_all.at[b], b, u_parts(1, 2), 0, cols)
-    for k in range(2, len(order)):
+    accumulate(acc, u_all.at[b], b, u_parts(2, 3), 0, cols)
+    relay_u(6)
+    for k in range(4, len(order)):
         u_copy(1, *order[k]).wait_recv()
-    accumulate(acc, u_all.at[sibling], sibling, u_parts(1, 2), 0, cols)
-    relay_u(4)
+    accumulate(acc, u_all.at[sibling], sibling, u_parts(2, 3), 0, cols)
     s_copy().wait_recv()
     m_copy(0).start()
     m_copy(1).start()
-    relay_u(5)
-    accumulate(acc, u_all.at[across], across, u_parts(1, 2), other * half, half)
-    for k in range(2, len(order)):
+    most = [piece(t, 2), piece(t, 3), piece(other, 2)]
+    last = [piece(other, 3)]
+    accumulate(acc, u_all.at[across], across, most, other * half, half)
+    for k in range(4, len(order) - 1):
         u_copy(2, *order[k]).wait_recv()
+    accumulate(acc, u_all.at[diagonal], diagonal, most, other * half, half)
+    relay_u(7)
+    accumulate(acc, u_all.at[across], across, last, other * half, half)
+    u_copy(2, *order[7]).wait_recv()
+    accumulate(acc, u_all.at[diagonal], diagonal, last, other * half, half)
     for q in range(half // TILE):
         at = span(other * half + q * TILE, TILE)
-        accumulate(acc, u_all.at[diagonal], diagonal, u_parts(1, 2), other * half + q * TILE, TILE)
         to_task[:, q * TILE:(q + 1) * TILE] = coef * acc[:, at]
         f_copy(q).start()
-    accumulate(acc, u_all.at[across], across, u_parts(1, 2), t * half, half)
-    accumulate(acc, u_all.at[diagonal], diagonal, u_parts(1, 2), t * half, half)
+    alpha_row = look_up(alpha_table[...], alpha_index[...])
+    alpha_part[...] = jnp.broadcast_to(alpha_row, (128, rows)).T
+    accumulate(acc, u_all.at[across], across, u_parts(2, 3), t * half, half)
+    accumulate(acc, u_all.at[diagonal], diagonal, u_parts(2, 3), t * half, half)
     m_copy(0).wait_recv()
     m_copy(2).start()
     m_copy(1).wait_recv()
@@ -406,7 +436,7 @@
         at = span(t * half + q * TILE, TILE)
         within = pl.ds(q * TILE, TILE)
         diag = alpha_part[:, :1] + beta_part[:, within]
-        acc[:, at] = coef * acc[:, at] + product(square_stack[...], *halves(v_col[:, within])) + diag * v_ref[:, at]
+        acc[:, at] = coef * acc[:, at] + product(square_stack[...], *halves(v_col[:, within])) + diag * v_all[b, :, at]
     for q in range(half // TILE):
         f_copy(q).wait_recv()
         within = pl.ds(q * TILE, TILE)
@@ -451,11 +481,14 @@
     s_copy().wait_send()
 
 
-def scratch(na, nb, rows, cols, full_a):
+def scratch(na, nb, rows, cols, full_a, alpha_size, beta_size):
     quarter = full_a // nb
     eighth = quarter // 2
     half = cols // 2
     buffers = [
+        pltpu.VMEM((rows, full_a), F32),
+        pltpu.VMEM((alpha_size // 128, 128), F32),
+        pltpu.VMEM((beta_size // 128, 128), F32),
         pltpu.VMEM((2, STRIP, nb * cols), F32),
         pltpu.VMEM((cols, nb * cols), BF16),
         pltpu.VMEM((cols, nb * cols), BF16),
@@ -487,7 +520,7 @@
     tiles = half // TILE
     parts = len(pieces_of(half))
     counts = [
-        (2,), (parts, 3), (parts, 3), (parts, 2), (2,), (2,), (parts,), (parts,),
+        (4,), (2,), (parts, 3), (parts, 3), (parts, 2), (2,), (2,), (parts,), (parts,),
         (3,), (3,), (), (), (4,), (4,), (5,), (5,), (3, 2 * parts), (3, 2 * parts), (3,), (3,), (tiles,), (tiles,),
     ]
     return buffers, [dma(c) if c else dma for c in counts]
@@ -498,12 +531,13 @@
 ):
     na, nb = mesh.shape["alpha"], mesh.shape["beta"]
     rows, cols = vector.shape
-    buffers, semaphores = scratch(na, nb, rows, cols, alpha_rows.shape[1])
+    buffers, semaphores = scratch(na, nb, rows, cols, alpha_rows.shape[1], alpha_energy.size, beta_energy.size)
     vmem = pl.BlockSpec(memory_space=pltpu.VMEM)
+    whole = pl.BlockSpec(memory_space=pl.ANY)
     return pl.pallas_call(
         functools.partial(kernel, na, nb),
         out_shape=jax.ShapeDtypeStruct((rows, cols // 2), F32),
-        in_specs=[pl.BlockSpec(memory_space=pltpu.SMEM)] + [vmem] * 6 + [pl.BlockSpec(memory_space=pl.ANY)],
+        in_specs=[pl.BlockSpec(memory_space=pltpu.SMEM)] + [whole] * 4 + [vmem] * 2 + [whole],
         out_specs=vmem,
         scratch_shapes=buffers + semaphores,
         compiler_params=pltpu.CompilerParams(
@@ -523,9 +557,9 @@
         return False
     if alpha_energy.size % 128 or beta_energy.size % 128:
         return False
-    buffers, _ = scratch(na, nb, rows, cols, full_a)
+    buffers, _ = scratch(na, nb, rows, cols, full_a, alpha_energy.size, beta_energy.size)
     size = sum(buf.dtype.itemsize * functools.reduce(lambda x, y: x * y, buf.shape) for buf in buffers)
-    size += 4 * (rows * cols + rows * full_a + rows * cols // 2)
+    size += 2 * rows * cols
     return size < VMEM_BUDGET
 
 

time: 84.6 us -> 75.9 us (0.90)
  Pallas kernels: 82.5 us -> 73.8 us
    pallas_call x1, Pallas kernels: 82.5 us -> 73.8 us  [fused(): pl.pallas_call(functools.partial(kernel, na, nb), out_shape=jax.ShapeDtyp...]
where the time goes in v2:
time: 75.9 us; the launch traced here: 75.7 us
  Pallas kernels  73.8 us (97%)
  local copies, waits for them, and re-layouts  1.87 us (2%)
    pallas_call x1, Pallas kernels, fused(): pl.pallas_call(functools.partial(kernel, na, nb), out_shape=jax.ShapeDtyp...  73.8 us
    unnamed x1, local copies, waits for them, and re-layouts  1.87 us

profile of v2, /device:TPU:0, one launch (start us, length us, event | category | flops | bytes accessed | tf_op | source)
XLA Modules:
  0.0 75.7 jit_solution(5919498273396954432)
XLA Ops:
  0.0 73.8 %shard_map.82 = f32[256,512]{1,0:T(8,128)} custom-call(f32[2]{0:T(128)} %weight_ref.1, f32[256,1024]{1,0:T(8,128)} %v_hbm.1, f32[256,1024]{1,0:T(8,128)} %bitcast.7, f32[512,128]{1,0:T(8,128)} %bitcast.8, f32[512,128]{1,0:T(8,128)} %bitcast.9, s32[1,256]{1,0:T(1,128)} %bitcast.11, s32[1,1024]{1,0:T(1,128)} %bitcast.10, f32[1024,4096]{1,0:T(8,128)} %bitcast.6), custom_call_target="tpu_custom_call" | custom-call | tf_op jit(solution)/shard_map/pallas_call | solution.py:537
  73.8 1.9 %copy.10 = f32[256,512]{1,0:T(8,128)} copy(f32[256,512]{1,0:T(8,128)} %shard_map.82) | data formatting | bytes 1048576

commit v3 on v2

--- a/solution.py
+++ b/solution.py
@@ -154,15 +154,27 @@
         where = {"beta": across} if n == 0 else {"beta": sibling}
         return remote(ref, ref, u_send.at[n, k], u_recv.at[n, k], where)
 
-    far = span(rows * jnp.where(a == 0, 1, 0), (na - 1) * rows)
-    far_pair = span(rows * jnp.where(a < 2, 2, 0), 2 * rows)
+    def block_of(n):
+        return (3 - a, lax.rem(a + 2, 4), peer(1), lax.rem(a + 2, 4), 3 - a)[n]
+
+    def gram_block(ref, i):
+        return ref.at[:, block_span(i, rows)]
 
     def e_copy(n):
-        if n == 0:
-            return remote(gram.at[:, far], gram_end.at[:, far], e_send.at[0], e_recv.at[0], {"alpha": peer(1)})
-        if n == 1:
-            return remote(sum_out, sum_in, e_send.at[1], e_recv.at[1], {"alpha": peer(3)})
-        return remote(last_out, last_in, e_send.at[2], e_recv.at[2], {"alpha": peer(1)})
+        if n < 3:
+            return remote(
+                gram_block(gram, block_of(n)), gram_block(gram_end, block_of(n)),
+                e_send.at[n], e_recv.at[n], {"alpha": peer(1)},
+            )
+        if n < 5:
+            return remote(sum_out.at[n - 3], sum_in.at[n - 3], e_send.at[n], e_recv.at[n], {"alpha": peer(3)})
+        return remote(last_out, last_in, e_send.at[n], e_recv.at[n], {"alpha": peer(1)})
+
+    def forward_sum(n):
+        block = block_span(block_of(3 + n), rows)
+        e_copy(n).wait_recv()
+        sum_out[n] = gram[:, block] + gram_end[:, block]
+        e_copy(3 + n).start()
 
     def s_copy():
         ref = square.at[:, span(b * quarter + t * eighth, eighth)]
@@ -334,7 +346,8 @@
 
     @pl.when(outer)
     def _():
-        e_copy(0).start()
+        for n in range(3):
+            e_copy(n).start()
 
     v_copy(2).wait_recv()
     v_relay(2).start()
@@ -360,55 +373,61 @@
     beta_part[...] = look_up(beta_table[...], beta_index[:, span(t * half, half)])
     relay_u(1)
     make_u(other, 1)
-    accumulate(acc, u_all.at[b], b, u_parts(0, 1), 0, cols, True)
+
+    @pl.when(inner)
+    def _():
+        forward_sum(0)
+
+    accumulate(acc, u_all.at[b], b, u_parts(0, 1), other * half, half, True)
     project(2)
     make_u(t, 2)
     for k in range(4):
         u_copy(1, *order[k]).wait_recv()
-    accumulate(acc, u_all.at[sibling], sibling, u_parts(0, 1), 0, cols)
+    accumulate(acc, u_all.at[sibling], sibling, u_parts(0, 1), other * half, half)
     relay_u(2)
 
     @pl.when(inner)
     def _():
-        e_copy(0).wait_recv()
-        sum_out[...] = gram[:, far_pair] + gram_end[:, far_pair]
-        e_copy(1).start()
+        forward_sum(1)
 
     relay_u(3)
+
+    @pl.when(inner)
+    def _():
+        e_copy(3).wait_recv()
+        last_out[...] = gram[:, block_span(peer(1), rows)] + sum_in[0]
+        e_copy(5).start()
+
     make_u(other, 2)
     project(3)
     make_u(t, 3)
-    accumulate(acc, u_all.at[across], across, u_parts(0, 1), 0, cols)
+    accumulate(acc, u_all.at[across], across, u_parts(0, 1), other * half, half)
     relay_u(4)
-
-    @pl.when(inner)
-    def _():
-        e_copy(1).wait_recv()
-        last_out[...] = gram[:, block_span(peer(1), rows)] + sum_in[:, block_span(a - 1, rows)]
-        e_copy(2).start()
-        kept = gram[:, block_span(a, rows)] + (gram_end[:, block_span(a, rows)] + sum_in[:, block_span(2 - a, rows)])
-        square[:, span(b * quarter + t * eighth, eighth)] = kept.T
 
     for k in range(4):
         u_copy(2, *order[k]).wait_recv()
-    accumulate(acc, u_all.at[diagonal], diagonal, u_parts(0, 1), 0, cols)
+    accumulate(acc, u_all.at[diagonal], diagonal, u_parts(0, 1), other * half, half)
     make_u(other, 3)
     relay_u(5)
+    accumulate(acc, u_all.at[b], b, u_parts(2, 3), other * half, half)
+
+    @pl.when(inner)
+    def _():
+        e_copy(2).wait_recv()
+        e_copy(4).wait_recv()
+        own = block_span(a, rows)
+        square[:, span(b * quarter + t * eighth, eighth)] = (gram[:, own] + (gram_end[:, own] + sum_in[1])).T
 
     @pl.when(outer)
     def _():
-        e_copy(2).wait_recv()
+        e_copy(5).wait_recv()
         square[:, span(b * quarter + t * eighth, eighth)] = (gram[:, block_span(a, rows)] + last_in[...]).T
 
     s_copy().start()
-    accumulate(acc, u_all.at[b], b, u_parts(2, 3), 0, cols)
     relay_u(6)
     for k in range(4, len(order)):
         u_copy(1, *order[k]).wait_recv()
-    accumulate(acc, u_all.at[sibling], sibling, u_parts(2, 3), 0, cols)
-    s_copy().wait_recv()
-    m_copy(0).start()
-    m_copy(1).start()
+    accumulate(acc, u_all.at[sibling], sibling, u_parts(2, 3), other * half, half)
     most = [piece(t, 2), piece(t, 3), piece(other, 2)]
     last = [piece(other, 3)]
     accumulate(acc, u_all.at[across], across, most, other * half, half)
@@ -425,8 +444,12 @@
         f_copy(q).start()
     alpha_row = look_up(alpha_table[...], alpha_index[...])
     alpha_part[...] = jnp.broadcast_to(alpha_row, (128, rows)).T
-    accumulate(acc, u_all.at[across], across, u_parts(2, 3), t * half, half)
-    accumulate(acc, u_all.at[diagonal], diagonal, u_parts(2, 3), t * half, half)
+    s_copy().wait_recv()
+    m_copy(0).start()
+    m_copy(1).start()
+    accumulate(acc, u_all.at[b], b, whole, t * half, half, True)
+    for block in (sibling, across, diagonal):
+        accumulate(acc, u_all.at[block], block, whole, t * half, half)
     m_copy(0).wait_recv()
     m_copy(2).start()
     m_copy(1).wait_recv()
@@ -460,12 +483,13 @@
 
     @pl.when(outer)
     def _():
-        e_copy(0).wait_send()
+        for n in range(3):
+            e_copy(n).wait_send()
 
     @pl.when(inner)
     def _():
-        e_copy(1).wait_send()
-        e_copy(2).wait_send()
+        for n in range(3, 6):
+            e_copy(n).wait_send()
 
     a_copy().wait_send()
     a_relay().wait_send()
@@ -505,8 +529,8 @@
         pltpu.VMEM((nb, rows, cols), F32),
         pltpu.VMEM((eighth, full_a), F32),
         pltpu.VMEM((eighth, full_a), F32),
-        pltpu.VMEM((eighth, 2 * rows), F32),
-        pltpu.VMEM((eighth, 2 * rows), F32),
+        pltpu.VMEM((2, eighth, rows), F32),
+        pltpu.VMEM((2, eighth, rows), F32),
         pltpu.VMEM((eighth, rows), F32),
         pltpu.VMEM((eighth, rows), F32),
         pltpu.VMEM((rows, full_a), F32),
@@ -521,7 +545,7 @@
     parts = len(pieces_of(half))
     counts = [
         (4,), (2,), (parts, 3), (parts, 3), (parts, 2), (2,), (2,), (parts,), (parts,),
-        (3,), (3,), (), (), (4,), (4,), (5,), (5,), (3, 2 * parts), (3, 2 * parts), (3,), (3,), (tiles,), (tiles,),
+        (6,), (6,), (), (), (4,), (4,), (5,), (5,), (3, 2 * parts), (3, 2 * parts), (3,), (3,), (tiles,), (tiles,),
     ]
     return buffers, [dma(c) if c else dma for c in counts]
 

time: 75.9 us -> 73 us (0.962)
  Pallas kernels: 73.8 us -> 70.9 us
    pallas_call x1, Pallas kernels: 73.8 us -> 70.9 us  [fused(): pl.pallas_call(functools.partial(kernel, na, nb), out_shape=jax.ShapeDtyp...]
where the time goes in v3:
time: 73 us; the launch traced here: 72.8 us
  Pallas kernels  70.9 us (97%)
  local copies, waits for them, and re-layouts  1.87 us (3%)
    pallas_call x1, Pallas kernels, fused(): pl.pallas_call(functools.partial(kernel, na, nb), out_shape=jax.ShapeDtyp...  70.9 us
    unnamed x1, local copies, waits for them, and re-layouts  1.87 us

profile of v3, /device:TPU:0, one launch (start us, length us, event | category | flops | bytes accessed | tf_op | source)
XLA Modules:
  0.0 72.8 jit_solution(1831431870055142044)
XLA Ops:
  0.0 70.9 %shard_map.82 = f32[256,512]{1,0:T(8,128)} custom-call(f32[2]{0:T(128)} %weight_ref.1, f32[256,1024]{1,0:T(8,128)} %v_hbm.1, f32[256,1024]{1,0:T(8,128)} %bitcast.7, f32[512,128]{1,0:T(8,128)} %bitcast.8, f32[512,128]{1,0:T(8,128)} %bitcast.9, s32[1,256]{1,0:T(1,128)} %bitcast.11, s32[1,1024]{1,0:T(1,128)} %bitcast.10, f32[1024,4096]{1,0:T(8,128)} %bitcast.6), custom_call_target="tpu_custom_call" | custom-call | tf_op jit(solution)/shard_map/pallas_call | solution.py:561
  70.9 1.9 %copy.10 = f32[256,512]{1,0:T(8,128)} copy(f32[256,512]{1,0:T(8,128)} %shard_map.82) | data formatting | bytes 1048576

commit v4 on v3

--- a/solution.py
+++ b/solution.py
@@ -53,9 +53,9 @@
 
 
 def kernel(
-    na, nb, weight_ref, v_hbm, a_hbm, alpha_hbm, beta_hbm, alpha_index, beta_index, b_hbm, out_ref,
+    na, nb, weight_ref, v_hbm, a_hbm, alpha_hbm, beta_hbm, alpha_index, beta_index, b_hbm, own_out, from_task,
     a_ref, alpha_table, beta_table, strip, b_high, b_low, v_all, v_col, a_other, a_stack, stack, total, acc, p_own, ret_out, ret_in, u_all,
-    gram, gram_end, sum_out, sum_in, last_out, last_in, square, square_stack, from_task, to_task,
+    gram, gram_end, sum_out, sum_in, last_out, last_in, square, square_stack, to_task,
     alpha_part, beta_part,
     local_sem, strip_sem, z_send, z_recv, r_send, a_send, a_recv, p_send, p_recv,
     e_send, e_recv, s_send, s_recv, v_send, v_recv, k_send, k_recv, u_send, u_recv, m_send, m_recv, f_send, f_recv,
@@ -188,6 +188,10 @@
     def f_copy(q):
         at = pl.ds(q * TILE, TILE)
         return remote(to_task.at[:, at], from_task.at[:, at], f_send.at[q], f_recv.at[q], {"task": other})
+
+    def own_copy(q):
+        at = span(t * half + q * TILE, TILE)
+        return pltpu.make_async_copy(acc.at[:, at], own_out.at[:, pl.ds(q * TILE, TILE)], local_sem.at[q])
 
     strips = cols // STRIP
 
@@ -460,10 +464,10 @@
         within = pl.ds(q * TILE, TILE)
         diag = alpha_part[:, :1] + beta_part[:, within]
         acc[:, at] = coef * acc[:, at] + product(square_stack[...], *halves(v_col[:, within])) + diag * v_all[b, :, at]
+        own_copy(q).start()
     for q in range(half // TILE):
+        own_copy(q).wait()
         f_copy(q).wait_recv()
-        within = pl.ds(q * TILE, TILE)
-        out_ref[:, within] = acc[:, span(t * half + q * TILE, TILE)] + from_task[:, within]
 
     for q in range(half // TILE):
         f_copy(q).wait_send()
@@ -536,7 +540,6 @@
         pltpu.VMEM((rows, full_a), F32),
         pltpu.VMEM((2 * rows, full_a), BF16),
         pltpu.VMEM((rows, half), F32),
-        pltpu.VMEM((rows, half), F32),
         pltpu.VMEM((rows, 128), F32),
         pltpu.VMEM((1, half), F32),
     ]
@@ -544,7 +547,7 @@
     tiles = half // TILE
     parts = len(pieces_of(half))
     counts = [
-        (4,), (2,), (parts, 3), (parts, 3), (parts, 2), (2,), (2,), (parts,), (parts,),
+        (max(4, tiles),), (2,), (parts, 3), (parts, 3), (parts, 2), (2,), (2,), (parts,), (parts,),
         (6,), (6,), (), (), (4,), (4,), (5,), (5,), (3, 2 * parts), (3, 2 * parts), (3,), (3,), (tiles,), (tiles,),
     ]
     return buffers, [dma(c) if c else dma for c in counts]
@@ -558,11 +561,11 @@
     buffers, semaphores = scratch(na, nb, rows, cols, alpha_rows.shape[1], alpha_energy.size, beta_energy.size)
     vmem = pl.BlockSpec(memory_space=pltpu.VMEM)
     whole = pl.BlockSpec(memory_space=pl.ANY)
-    return pl.pallas_call(
+    own, received = pl.pallas_call(
         functools.partial(kernel, na, nb),
-        out_shape=jax.ShapeDtypeStruct((rows, cols // 2), F32),
+        out_shape=[jax.ShapeDtypeStruct((rows, cols // 2), F32)] * 2,
         in_specs=[pl.BlockSpec(memory_space=pltpu.SMEM)] + [whole] * 4 + [vmem] * 2 + [whole],
-        out_specs=vmem,
+        out_specs=[whole] * 2,
         scratch_shapes=buffers + semaphores,
         compiler_params=pltpu.CompilerParams(
             collective_id=0, has_side_effects=True, vmem_limit_bytes=60 * 1024 * 1024
@@ -571,6 +574,7 @@
         op_weight, vector, alpha_rows, alpha_energy.reshape(-1, 128), beta_energy.reshape(-1, 128),
         alpha_string.reshape(1, -1), beta_string.reshape(1, -1), beta_rows,
     )
+    return own + received
 
 
 def fits(mesh, vector, alpha_rows, alpha_energy, beta_energy):

time: 73 us -> 72.4 us (level)
  other arithmetic: 0 us -> 2.07 us
  local copies, waits for them, and re-layouts: 1.87 us -> 0 us
  Pallas kernels: 70.9 us -> 70.1 us
    add x0 -> x1, other arithmetic: none -> 2.07 us  [fused(): return own + received]
    unnamed x1 -> x0, local copies, waits for them, and re-layouts: 1.87 us -> none
    pallas_call x1, Pallas kernels: 70.9 us -> 70.1 us  [fused(): pl.pallas_call(functools.partial(kernel, na, nb), out_shape=[jax.ShapeDty...]
where the time goes in v4:
time: 72.4 us; the launch traced here: 72.2 us
  Pallas kernels  70.1 us (97%)
  other arithmetic  2.07 us (3%)
    pallas_call x1, Pallas kernels, fused(): pl.pallas_call(functools.partial(kernel, na, nb), out_shape=[jax.ShapeDty...  70.1 us
    add x1, other arithmetic, fused(): return own + received  2.07 us

profile of v4, /device:TPU:0, one launch (start us, length us, event | category | flops | bytes accessed | tf_op | source)
XLA Modules:
  0.0 72.2 jit_solution(9638104169855225639)
XLA Ops:
  0.0 70.1 %shard_map.82 = (f32[256,512]{1,0:T(8,128)}, f32[256,512]{1,0:T(8,128)}) custom-call(f32[2]{0:T(128)} %weight_ref.1, f32[256,1024]{1,0:T(8,128)} %v_hbm.1, f32[256,1024]{1,0:T(8,128)} %bitcast.7, f32[512,128]{1,0:T(8,128)} %bitcast.8, f32[512,128]{1,0:T(8,128)} %bitcast.9, s32[1,256]{1,0:T(1,128)} %bitcast.11, s32[1,1024]{1,0:T(1,128)} %bitcast.10, ...), custom_call_target="tpu_custom_call" | custom-call | tf_op jit(solution)/shard_map/pallas_call | solution.py:564
  70.2 2.1 %add.3 = f32[256,512]{1,0:T(8,128)} add(f32[256,512]{1,0:T(8,128)} %get-tuple-element.7, f32[256,512]{1,0:T(8,128)} %get-tuple-element.8) | non-fusion elementwise | flops 131072 | bytes 1572864 | tf_op jit(solution)/shard_map/add | solution.py:577
